TPU v7x, 128 devices: a whole 4x4x4 slice. The times are simulated.
128 devices in a mesh: slab: 32 (over y, x, core), mp: 4 (over z).
Axes of the slice: x: 4, y: 4, z: 4, core: 2. Of those that a mesh axis runs over, the one named last changes fastest.
Arguments:
- velocity: float32 [3, 256, 512, 256], P(None, 'slab', 'mp'), may hold values from -6 to 6
- anchors: int32 [3, 32, 4, 256], P(None, 'slab', 'mp'), may hold values from 0 to 504, as said below
- dest: int32 [32, 4, 256, 1], P('slab', 'mp'), may hold values from 0 to 31; in each aligned block of 256 rows (0 to 255, 256 to 511, ..., all dimensions but the last counted through in order) at most 16 rows name the same one
- w_lift: bfloat16 [1536, 512], replicated, may hold values from -0.15625 to 0.15625
- w_query: bfloat16 [512, 512], P(None, 'mp'), may hold values from -0.25 to 0.25
- w_key: bfloat16 [512, 512], P(None, 'mp'), may hold values from -0.25 to 0.25
- w_value: bfloat16 [512, 512], P(None, 'mp'), may hold values from -0.25 to 0.25
- w_out: bfloat16 [512, 512], P('mp'), may hold values from -0.25 to 0.25
- w_proj: bfloat16 [512, 1536], replicated, may hold values from -0.25 to 0.25
Outputs:
- new_velocity: float32 [3, 256, 512, 256], P(None, 'slab', 'mp')
- loss: float32 [], replicated
- g_lift: float32 [1536, 512], P('slab')
- g_query: float32 [512, 512], P(None, 'mp')
- g_key: float32 [512, 512], P(None, 'mp')
- g_value: float32 [512, 512], P(None, 'mp')
- g_out: float32 [512, 512], P('mp')
- g_proj: float32 [512, 1536], P('slab')
Inputs may be any that keep to these rules, and one draw needn't show every extreme that they name: Each device's 256 anchors are distinct, multiples of 8 in each coordinate (z, y, x along the first dimension), and name patches inside that device's own block of the grid. `dest`: among the 256 rows of one device no trainer shard is named more than 16 times, and in some device's rows some shard is named exactly 16 times; every shard is named by some row.
All inputs are finite; a program needn't handle non-finite values.
Results may differ from a plain program's by a relative error of at most 0.0035.
Values may be sent and summed in bfloat16 or wider, within the bound.
No kernel may reach another device: no remote copies, remote signals or barrier semaphores. Data moves between devices by JAX's collectives and lax.ppermute only.
A program may use at most 192 MiB of HBM per device.

v0:
```python
import jax
import jax.numpy as jnp
from jax import lax
from jax.sharding import PartitionSpec as P

HEAD_DIM = 64
TIME_STEP = 0.1
VISCOSITY = 0.2
EPSILON = 1e-05
EXACT = lax.Precision.HIGHEST


def with_halo(shard, sides, width):
    for axis, dim in sides:
        devices, length = (lax.axis_size(axis), shard.shape[dim])
        up = [(i, (i + 1) % devices) for i in range(devices)]
        down = [(j, i) for i, j in up]
        last = lax.slice_in_dim(shard, length - width, length, axis=dim)
        first = lax.slice_in_dim(shard, 0, width, axis=dim)
        before = lax.ppermute(last, axis, up)
        after = lax.ppermute(first, axis, down)
        shard = jnp.concatenate([before, shard, after], axis=dim)
    return shard


def update(centre, z_next, z_prev, y_next, y_prev, x_next, x_prev):
    laplace = z_next + z_prev + y_next + y_prev + x_next + x_prev - 6.0 * centre
    transport = (
        centre[0:1] * (0.5 * (x_next - x_prev))
        + centre[1:2] * (0.5 * (y_next - y_prev))
        + centre[2:3] * (0.5 * (z_next - z_prev))
    )
    return centre - TIME_STEP * transport + VISCOSITY * TIME_STEP * laplace


def cut_patches(field):
    comps, size_z, size_y, size_x = field.shape
    blocks = field.reshape(comps, size_z // 8, 8, size_y // 8, 8, size_x // 8, 8)
    return blocks.transpose(1, 3, 5, 0, 2, 4, 6).reshape(-1, comps * 512)


def rounded(values):
    return lax.optimization_barrier(values.astype(jnp.bfloat16)).astype(jnp.float32)


def normalize(heads):
    centre = jnp.mean(heads, axis=-1, keepdims=True)
    shifted = heads - centre
    spread = jnp.sqrt(jnp.mean(shifted * shifted, axis=-1, keepdims=True) + EPSILON)
    return (shifted / spread, spread)


def norm_back(grad, normed, spread):
    inner = jnp.mean(grad, axis=-1, keepdims=True)
    cross = jnp.mean(grad * normed, axis=-1, keepdims=True)
    return (grad - inner - normed * cross) / spread


def shards(velocity, anchors, dest, w_lift, w_query, w_key, w_value, w_out, w_proj):
    padded = with_halo(velocity, (("slab", 1), ("mp", 2)), 1)
    centre = padded[:, 1:-1, 1:-1, :]
    new_velocity = update(
        centre,
        padded[:, 2:, 1:-1, :],
        padded[:, :-2, 1:-1, :],
        padded[:, 1:-1, 2:, :],
        padded[:, 1:-1, :-2, :],
        jnp.roll(centre, -1, 3),
        jnp.roll(centre, 1, 3),
    )
    size_z = velocity.shape[1]
    size_y = velocity.shape[2]
    size_x = velocity.shape[3]
    flat = anchors.reshape(3, -1)
    local_z = (flat[0] - lax.axis_index("slab") * size_z) // 8
    local_y = (flat[1] - lax.axis_index("mp") * size_y) // 8
    index = (local_z * (size_y // 8) + local_y) * (size_x // 8) + flat[2] // 8
    picked_old = cut_patches(velocity.astype(jnp.bfloat16))[index]
    picked_new = cut_patches(new_velocity.astype(jnp.bfloat16))[index]
    target = dest.reshape(-1)
    chosen = target.shape[0]
    groups = lax.axis_size("slab")
    token_total = groups * lax.axis_size("mp") * chosen
    width = picked_old.shape[1]
    capacity = max(2, 2 * chosen // groups)
    hits = (target[:, None] == jnp.arange(groups, dtype=jnp.int32)[None, :]).astype(jnp.int32)
    placing = jnp.sum(jnp.cumsum(hits, axis=0) * hits, axis=1) - 1
    slot = target * capacity + placing
    send_old = jnp.zeros((groups * capacity, width), jnp.bfloat16).at[slot].set(picked_old)
    send_new = jnp.zeros((groups * capacity, width), jnp.bfloat16).at[slot].set(picked_new)
    send_tag = (
        jnp.zeros((groups * capacity,), jnp.bfloat16)
        .at[slot]
        .set(jnp.ones((chosen,), jnp.bfloat16))
    )
    recv_old, recv_new, recv_tag = (
        lax.all_to_all(send_old, "slab", split_axis=0, concat_axis=0, tiled=True),
        lax.all_to_all(send_new, "slab", split_axis=0, concat_axis=0, tiled=True),
        lax.all_to_all(send_tag, "slab", split_axis=0, concat_axis=0, tiled=True),
    )
    valid_own = (recv_tag > 0).astype(jnp.float32)
    lifted_own = jnp.dot(recv_old, w_lift, preferred_element_type=jnp.float32).astype(jnp.bfloat16)
    tokens, tags = (
        lax.all_gather(lifted_own, "mp", axis=0, tiled=True),
        lax.all_gather(recv_tag, "mp", axis=0, tiled=True),
    )
    query_w, key_w, value_w, out_w = (w_query, w_key, w_value, w_out)
    total = tokens.shape[0]
    local_heads = query_w.shape[1] // HEAD_DIM
    shape = (total, local_heads, HEAD_DIM)
    queries = rounded(jnp.dot(tokens, query_w, preferred_element_type=jnp.float32).reshape(shape))
    keys_hat, key_spread = normalize(
        jnp.dot(tokens, key_w, preferred_element_type=jnp.float32).reshape(shape)
    )
    values_hat, value_spread = normalize(
        jnp.dot(tokens, value_w, preferred_element_type=jnp.float32).reshape(shape)
    )
    keys_round = rounded(keys_hat)
    values_round = rounded(values_hat)
    valid = (tags > 0).astype(jnp.float32)
    partial_sum = jnp.einsum(
        "thi,thj->hij", keys_round * valid[:, None, None], values_round, precision=EXACT
    )
    count = jnp.sum(valid)
    summary = partial_sum / count
    attended = jnp.einsum("thi,hij->thj", queries, summary, precision=EXACT)
    attended = attended.astype(jnp.bfloat16).reshape(total, -1)
    rows = attended
    mixed = lax.psum_scatter(
        jnp.dot(rows, out_w, preferred_element_type=jnp.float32),
        "mp",
        scatter_dimension=0,
        tiled=True,
    )
    hidden = (lifted_own.astype(jnp.float32) + mixed).astype(jnp.bfloat16)
    guess = jnp.dot(hidden, w_proj, preferred_element_type=jnp.float32)
    error = (guess - recv_new.astype(jnp.float32)) * valid_own[:, None]
    loss_part = jnp.sum(error * error) / (token_total * width)
    d_guess = (error / token_total).astype(jnp.bfloat16)
    g_proj = jnp.einsum("td,tf->df", hidden, d_guess, preferred_element_type=jnp.float32)
    d_hidden = jnp.einsum("tf,df->td", d_guess, w_proj, preferred_element_type=jnp.float32)
    d_tokens = lax.all_gather(d_hidden.astype(jnp.bfloat16), "mp", axis=0, tiled=True)
    g_out_turned = jnp.einsum("td,ta->da", d_tokens, attended, preferred_element_type=jnp.float32)
    d_attended = jnp.einsum(
        "td,ad->ta", d_tokens, out_w, preferred_element_type=jnp.float32
    ).reshape(shape)
    d_query = jnp.einsum("thj,hij->thi", d_attended, summary, precision=EXACT)
    partial_grad = jnp.einsum("thi,thj->hij", queries, d_attended, precision=EXACT)
    d_summary = partial_grad / count
    d_keys_hat = (
        jnp.einsum("thj,hij->thi", values_round, d_summary, precision=EXACT) * valid[:, None, None]
    )
    d_values_hat = (
        jnp.einsum("thi,hij->thj", keys_round, d_summary, precision=EXACT) * valid[:, None, None]
    )
    d_query = d_query.astype(jnp.bfloat16).reshape(total, -1)
    d_keys = norm_back(d_keys_hat, keys_hat, key_spread).astype(jnp.bfloat16).reshape(total, -1)
    d_values = (
        norm_back(d_values_hat, values_hat, value_spread).astype(jnp.bfloat16).reshape(total, -1)
    )
    g_query = jnp.einsum("td,ta->da", tokens, d_query, preferred_element_type=jnp.float32)
    g_key = jnp.einsum("td,ta->da", tokens, d_keys, preferred_element_type=jnp.float32)
    g_value = jnp.einsum("td,ta->da", tokens, d_values, preferred_element_type=jnp.float32)
    stacked = jnp.concatenate([d_query, d_keys, d_values], axis=1)
    weights = jnp.concatenate([query_w, key_w, value_w], axis=1)
    rows = stacked
    d_lifted = (
        d_hidden
        + lax.psum_scatter(
            jnp.einsum("ta,da->td", rows, weights, preferred_element_type=jnp.float32),
            "mp",
            scatter_dimension=0,
            tiled=True,
        )
    ).astype(jnp.bfloat16)
    g_out = g_out_turned.T
    g_lift = jnp.einsum("tf,td->fd", recv_old, d_lifted, preferred_element_type=jnp.float32)
    g_query, g_key, g_value, g_out = lax.psum((g_query, g_key, g_value, g_out), "slab")
    g_lift, g_proj, loss = lax.psum((g_lift, g_proj, loss_part), ("slab", "mp"))
    slab_at = lax.axis_index("slab")
    lift_rows = g_lift.shape[0] // groups
    proj_rows = g_proj.shape[0] // groups
    g_lift = lax.dynamic_slice_in_dim(g_lift, slab_at * lift_rows, lift_rows, 0)
    g_proj = lax.dynamic_slice_in_dim(g_proj, slab_at * proj_rows, proj_rows, 0)
    return (new_velocity, loss, g_lift, g_query, g_key, g_value, g_out, g_proj)


def solution(mesh):
    return jax.shard_map(
        shards,
        mesh=mesh,
        in_specs=(
            P(None, "slab", "mp", None),
            P(None, "slab", "mp", None),
            P("slab", "mp", None, None),
            P(),
            P(None, "mp"),
            P(None, "mp"),
            P(None, "mp"),
            P("mp", None),
            P(),
        ),
        out_specs=(
            P(None, "slab", "mp", None),
            P(),
            P("slab", None),
            P(None, "mp"),
            P(None, "mp"),
            P(None, "mp"),
            P("mp", None),
            P("slab", None),
        ),
        check_vma=False,
    )
```

profile of v0, /device:TPU:6, one launch (start us, length us, event | category | flops | bytes accessed | tf_op | source)
XLA Modules:
  0.0 671.7 jit_solution(10463067455950376198)
XLA Ops:
  7.2 2.1 fusion.47
  13.0 3.5 collective-permute-done
  17.3 5.1 fusion.44
  22.4 30.4 %reshape.376 = bf16[3,1,8,16,8,32,8]{6,5,4,3,2,0,1:T(8,128)(2,1)} reshape(bf16[3,8,128,256]{3,2,1,0:T(8,128)(2,1)S(1)} %get-tuple-element.22) | data formatting | bytes 3145728 | tf_op jit(solution)/shard_map/reshape | solution.py:38
  52.8 22.7 %copy.29 = bf16[1,16,32,3,8,8,8]{2,1,6,5,4,3,0:T(8,128)(2,1)} copy(bf16[1,16,32,3,8,8,8]{6,2,5,1,4,3,0:T(8,128)(2,1)} %bitcast.157) | data formatting | bytes 3145728 | tf_op jit(solution)/shard_map/transpose | solution.py:39
  75.5 8.4 %reshape.377 = bf16[512,1536]{0,1:T(8,128)(2,1)S(1)} reshape(bf16[1,16,32,3,8,8,8]{2,1,6,5,4,3,0:T(8,128)(2,1)} %copy.29) | data formatting | bytes 3145728 | tf_op jit(solution)/shard_map/reshape | solution.py:39
  83.8 1.6 copy.30
  85.4 5.3 scatter_custom_fusion
  90.8 28.1 %all_to_all.34 = bf16[32,16,1536]{2,1,0:T(8,128)(2,1)S(1)} all-to-all(bf16[32,16,1536]{2,1,0:T(8,128)(2,1)S(1)} %bitcast.164), channel_id=1, replica_groups=mesh['slab'=32,'mp'=4] {'slab'}, dimensions={0} | all-to-all | bytes 3145728 | tf_op jit(solution)/shard_map/all_to_all | solution.py:97
  120.0 1.8 convolution_convert_fusion.3
  121.9 2.2 scatter_custom_fusion.1
  124.1 11.3 %all_to_all.35 = bf16[32,16,1]{1,2,0:T(2,128)(2,1)S(1)} all-to-all(bf16[32,16,1]{1,2,0:T(2,128)(2,1)S(1)} %all_to_all.30), channel_id=1, replica_groups=mesh['slab'=32,'mp'=4] {'slab'}, dimensions={0} | all-to-all | bytes 2048 | tf_op jit(solution)/shard_map/all_to_all | solution.py:99
  135.5 12.8 %all-gather = bf16[4,1,512]{2,1,0:T(2,128)(2,1)S(1)} all-gather(bf16[1,1,512]{2,1,0:T(2,128)(2,1)S(1)} %reshape.428), channel_id=1, replica_groups=mesh['slab'=32,'mp'=4] {'mp'}, dimensions={0}, use_global_device_ids=true | all-gather | bytes 5120 | tf_op jit(solution)/shard_map/all_gather | solution.py:105
  149.5 4.2 all-gather.4.cloned.1.call-done
  153.8 2.6 convolution_convert_fusion.2
  156.4 1.8 bitcast_reduce_fusion.1
  163.3 2.7 fusion.49
  166.2 4.1 fusion.45
  176.3 1.9 collective-permute-done.2
  178.3 2.3 collective-permute-done.3
  180.6 9.0 %fusion.42 = (bf16[3,8,128,256]{3,2,1,0:T(8,128)(2,1)}, f32[3,8,128,256]{3,2,1,0:T(8,128)}) fusion(f32[3,8,128,256]{3,2,1,0:T(8,128)S(1)} %copy-done.1, f32[8,128,256]{2,1,0:T(8,128)S(1)} %get-tuple-element.29, f32[3,1,128,256]{3,2,1,0:T(8,128)S(1)} %collective-permute-done, f32[3,1,128,256]{3,2,1,0:T(8,128)} %copy-done.17, ...), kind=kLoop, calls=%fused_computation.120 | loop fusion | flops 20447232 | bytes 22081536 | tf_op jit(solution)/shard_map/convert_element_type | solution.py:79
  189.6 32.0 %reshape.381 = bf16[3,1,8,16,8,32,8]{6,5,4,3,2,0,1:T(8,128)(2,1)} reshape(bf16[3,8,128,256]{3,2,1,0:T(8,128)(2,1)} %get-tuple-element.18) | data formatting | bytes 3145728 | tf_op jit(solution)/shard_map/reshape | solution.py:38
  221.6 22.7 %copy.33 = bf16[1,16,32,3,8,8,8]{2,1,6,5,4,3,0:T(8,128)(2,1)} copy(bf16[1,16,32,3,8,8,8]{6,2,5,1,4,3,0:T(8,128)(2,1)} %bitcast.158) | data formatting | bytes 3145728 | tf_op jit(solution)/shard_map/transpose | solution.py:39
  244.3 9.3 %reshape.382 = bf16[512,1536]{0,1:T(8,128)(2,1)} reshape(bf16[1,16,32,3,8,8,8]{2,1,6,5,4,3,0:T(8,128)(2,1)} %copy.33) | data formatting | bytes 3145728 | tf_op jit(solution)/shard_map/reshape | solution.py:39
  253.6 2.6 copy.34
  256.2 6.3 scatter_custom_fusion.2
  262.5 10.4 %all-to-all-start.2 = ((bf16[32,16,1536]{2,1,0:T(8,128)(2,1)}), bf16[32,16,1536]{2,1,0:T(8,128)(2,1)}, u32[]{:S(2)}, u32[]{:S(2)}) async-start(bf16[32,16,1536]{2,1,0:T(8,128)(2,1)} %bitcast.163), calls=%async_computation.3 | async-start | bytes 3145728 | tf_op jit(solution)/shard_map/all_to_all | solution.py:98
  273.3 19.5 %all-to-all-done.2 = bf16[32,16,1536]{2,1,0:T(8,128)(2,1)} async-done(((bf16[32,16,1536]{2,1,0:T(8,128)(2,1)}), bf16[32,16,1536]{2,1,0:T(8,128)(2,1)}, u32[]{:S(2)}, u32[]{:S(2)}) %all-to-all-start.2) | async-done | bytes 1572896 | tf_op jit(solution)/shard_map/all_to_all | solution.py:98
  292.8 3.6 multiply_reduce_fusion
  296.5 2.2 fusion.48
  298.8 29.3 %all-gather.6.cloned.1.call-done = bf16[2048,512]{1,0:T(8,128)(2,1)} async-done(((bf16[512,512]{1,0:T(8,128)(2,1)}), bf16[2048,512]{1,0:T(8,128)(2,1)}) %all-gather.6.cloned.1.call-update) | async-done | bytes 2097168 | tf_op jit(solution)/shard_map/all_gather | solution.py:142
  328.1 2.5 fusion.50
  336.2 3.3 fusion.3
  339.5 5.2 fusion.19
  344.7 41.8 %reduce-scatter.5.cloned.1.call-done = f32[512,512]{1,0:T(8,128)} async-done(((f32[2048,512]{1,0:T(8,128)}), f32[512,512]{1,0:T(8,128)}) %reduce-scatter.5.cloned.1.call-update) | async-done | bytes 1048592 | tf_op jit(solution)/shard_map/reduce_scatter | solution.py:169
  386.6 4.2 fusion.21
  391.8 2.9 fusion.54
  394.7 3.1 fusion.51
  399.2 1.4 fusion.52
  401.4 65.5 %psum.49 = f32[]{:T(128)} all-reduce(f32[]{:T(128)S(6)} %div.119), channel_id=1, replica_groups=mesh['slab'=32,'mp'=4] {'slab','mp'}, use_global_device_ids=true, to_apply=%region_13.14 | all-reduce | flops 1 | bytes 8 | tf_op jit(solution)/shard_map/psum | solution.py:179
  466.8 81.8 %all-reduce.5.cloned.1.call-done = (f32[1536,512]{1,0:T(8,128)}, f32[512,1536]{1,0:T(8,128)}) async-done(((f32[1536,512]{1,0:T(8,128)}, f32[512,1536]{1,0:T(8,128)}), (f32[1536,512]{1,0:T(8,128)}, f32[512,1536]{1,0:T(8,128)})) %all-reduce.5.cloned.1.call-update) | async-done | bytes 6291472 | tf_op jit(solution)/shard_map/psum | solution.py:179
  548.6 1.5 constant_dynamic-slice_fusion.1
  550.1 1.5 constant_dynamic-slice_fusion
  551.7 106.2 %all-reduce.7.cloned.1.call-done = (f32[512,128]{1,0:T(8,128)}, f32[512,128]{1,0:T(8,128)}, f32[512,128]{1,0:T(8,128)}, f32[128,512]{1,0:T(8,128)}) async-done(((f32[512,128]{1,0:T(8,128)}, f32[512,128]{1,0:T(8,128)}, f32[512,128]{1,0:T(8,128)}, f32[128,512]{1,0:T(8,128)}), (f32[512,128]{1,0:T(8,128)}, f32[512,128]{1,0:T(8,128)}, f32[512,128]{1,0:T(8,128)}, ...) | async-done | bytes 1048592 | tf_op jit(solution)/shard_map/psum | solution.py:178
  657.9 1.7 copy.48
  659.6 1.7 copy.49
  661.2 1.7 copy.50
  662.9 1.7 copy.51
  (149 shorter events, 26.8 us)
Async XLA Ops:
  7.2 285.7 %copy-start = (bf16[512,1536]{1,0:T(8,128)(2,1)S(1)}, bf16[512,1536]{1,0:T(8,128)(2,1)}, u32[]{:S(2)}) copy-start(bf16[512,1536]{1,0:T(8,128)(2,1)} %param.17) | copy-start | bytes 4718596
  7.2 146.6 %all-gather.4.cloned.1.call-start = ((), (), s32[]{:S(2)}) async-start(), calls=%async_computation.5 | async-start | bytes 2621440 | tf_op jit(solution)/shard_map/all_gather | solution.py:104
  9.3 7.2 %collective-permute-start = (f32[3,1,128,256]{3,2,1,0:T(8,128)S(1)}, f32[3,1,128,256]{3,2,1,0:T(8,128)S(1)}, u32[]{:S(2)}, u32[]{:S(2)}) collective-permute-start(f32[3,1,128,256]{3,2,1,0:T(8,128)S(1)} %get-tuple-element.32), channel_id=1, source_target_pairs={{0,4},{4,8},{8,12},{12,16},{16,20},{20,24},{24,28},{28,32},{32,36}... | collective-permute-start | bytes 1179656 | tf_op jit(solution)/shard_map/ppermute | solution.py:20
  10.0 75.4 %copy-start.41 = (s32[1024]{0:T(1024)}, s32[1024]{0:T(1024)S(1)}, u32[]{:S(2)}) copy-start(s32[1024]{0:T(1024)S(1)} %pad_clamp_fusion) | copy-start | bytes 12292
  13.0 108.8 %copy-start.42 = (s32[256,1]{0,1:T(1,128)}, s32[256,1]{0,1:T(1,128)S(1)}, u32[]{:S(2)}) copy-start(s32[256,1]{0,1:T(1,128)S(1)} %compare_select_fusion.1) | copy-start | bytes 3076
  90.8 29.2 %copy-start.43 = (bf16[1536,512]{1,0:T(8,128)(2,1)S(1)}, bf16[1536,512]{1,0:T(8,128)(2,1)}, u32[]{:S(2)}) copy-start(bf16[1536,512]{1,0:T(8,128)(2,1)} %param.12) | copy-start | bytes 4718596
  118.8 34.9 %copy-start.37 = (bf16[512,128]{1,0:T(8,128)(2,1)S(1)}, bf16[512,128]{1,0:T(8,128)(2,1)}, u32[]{:S(2)}) copy-start(bf16[512,128]{1,0:T(8,128)(2,1)} %param.13) | copy-start | bytes 393220
  121.8 171.0 %reduce-scatter.3.cloned.1.call-start = ((), (), s32[]{:S(2)}) async-start(), calls=%async_computation.6 | async-start | bytes 5242880 | tf_op jit(solution)/shard_map/reduce_scatter | solution.py:129
  135.4 21.0 %copy-start.32 = (bf16[32,16,1]{1,2,0:T(2,128)(2,1)}, bf16[32,16,1]{1,2,0:T(2,128)(2,1)S(1)}, u32[]{:S(2)}) copy-start(bf16[32,16,1]{1,2,0:T(2,128)(2,1)S(1)} %all_to_all.35) | copy-start | bytes 3076
  153.8 2.6 copy-start.2
  156.4 2.2 copy-start.34
  158.4 2.1 copy-start.28
  158.5 3.3 copy-start.18
  158.5 2.0 copy-start.39
  159.4 3.9 copy-start.22
  159.4 3.1 copy-start.24
  160.3 2.2 copy-start.30
  160.5 2.0 copy-start.20
  166.0 4.3 copy-start.1
  166.0 5.8 collective-permute-start.1
  171.8 2.8 copy-start.17
  173.8 4.5 collective-permute-start.2
  174.6 6.0 collective-permute-start.3
  256.2 17.0 %copy-start.33 = (bf16[32,16,1]{1,2,0:T(2,128)(2,1)S(1)}, bf16[32,16,1]{1,2,0:T(2,128)(2,1)}, u32[]{:S(2)}) copy-start(bf16[32,16,1]{1,2,0:T(2,128)(2,1)} %copy-done.32) | copy-start | bytes 3076
  262.5 30.3 %all-to-all-start.2 = ((bf16[32,16,1536]{2,1,0:T(8,128)(2,1)}), bf16[32,16,1536]{2,1,0:T(8,128)(2,1)}, u32[]{:S(2)}, u32[]{:S(2)}) async-start(bf16[32,16,1536]{2,1,0:T(8,128)(2,1)} %bitcast.163), calls=%async_computation.3 | async-start | bytes 3145728 | tf_op jit(solution)/shard_map/all_to_all | solution.py:98
  272.9 55.1 %all-gather.6.cloned.1.call-start = ((), (), s32[]{:S(2)}) async-start(), calls=%async_computation.7 | async-start | bytes 2621440 | tf_op jit(solution)/shard_map/all_gather | solution.py:142
  296.5 2.2 copy-start.4
  296.5 31.6 %copy-start.23 = (bf16[128,512]{1,0:T(8,128)(2,1)S(1)}, bf16[128,512]{1,0:T(8,128)(2,1)}, u32[]{:S(2)}) copy-start(bf16[128,512]{1,0:T(8,128)(2,1)} %param.16) | copy-start | bytes 393220
  298.6 33.2 %copy-start.27 = (f32[2,64,64]{2,1,0:T(8,128)S(1)}, f32[2,64,64]{2,1,0:T(8,128)}, u32[]{:S(2)}) copy-start(f32[2,64,64]{2,1,0:T(8,128)} %copy-done.26) | copy-start | bytes 98308
  298.7 34.3 %copy-start.25 = (f32[2048,2]{0,1:T(2,128)S(1)}, f32[2048,2]{0,1:T(2,128)}, u32[]{:S(2)}) copy-start(f32[2048,2]{0,1:T(2,128)} %copy-done.24) | copy-start | bytes 49156
  298.7 34.3 %copy-start.31 = (f32[2048,2]{0,1:T(2,128)S(1)}, f32[2048,2]{0,1:T(2,128)}, u32[]{:S(2)}) copy-start(f32[2048,2]{0,1:T(2,128)} %copy-done.30) | copy-start | bytes 49156
  298.7 34.3 %copy-start.40 = (f32[4,1,512]{2,1,0:T(1,128)S(1)}, f32[4,1,512]{2,1,0:T(1,128)}, u32[]{:S(2)}) copy-start(f32[4,1,512]{2,1,0:T(1,128)} %compare_convert_fusion.1) | copy-start | bytes 24580
  298.7 87.8 %reduce-scatter.5.cloned.1.call-start = ((), (), s32[]{:S(2)}) async-start(), calls=%async_computation.8 | async-start | bytes 5242880 | tf_op jit(solution)/shard_map/reduce_scatter | solution.py:169
  328.1 4.9 copy-start.6
  328.1 4.9 copy-start.19
  331.9 2.0 copy-start.21
  331.9 2.0 copy-start.29
  333.0 2.4 copy-start.11
  334.7 1.5 copy-start.35
  334.7 1.5 copy-start.36
  334.7 1.4 copy-start.38
  339.5 47.1 %copy-start.8 = (bf16[32,16,1536]{2,1,0:T(8,128)(2,1)S(1)}, bf16[32,16,1536]{2,1,0:T(8,128)(2,1)}, u32[]{:S(2)}) copy-start(bf16[32,16,1536]{2,1,0:T(8,128)(2,1)} %copy-done.7) | copy-start | bytes 4718596
  339.5 209.1 %all-reduce.5.cloned.1.call-start = ((), (), s32[]{:S(2)}) async-start(), calls=%async_computation.9 | async-start | bytes 12582912 | tf_op jit(solution)/shard_map/psum | solution.py:179
  390.8 3.9 copy-start.12
  390.8 7.0 %copy-start.14 = (bf16[2048,2,64]{0,2,1:T(8,128)(2,1)S(1)}, bf16[2048,2,64]{0,2,1:T(8,128)(2,1)}, u32[]{:S(2)}) copy-start(bf16[2048,2,64]{0,2,1:T(8,128)(2,1)} %copy-done.13) | copy-start | bytes 1572868
  390.8 267.1 %all-reduce.7.cloned.1.call-start = ((), (), s32[]{:S(2)}) async-start(), calls=%async_computation.10 | async-start | bytes 2097152 | tf_op jit(solution)/shard_map/psum | solution.py:178
  391.8 6.0 copy-start.3
  394.7 4.6 copy-start.16
  (7 other events, 6.2 us)
Sparse Core Ops, SparseCore 0:
  121.9 31.8 all-gather.3
  166.1 47.4 reduce-scatter.2
  298.8 29.2 all-gather.5
  339.6 46.9 reduce-scatter.4
  391.3 157.2 all-reduce.4
  552.5 105.4 all-reduce.6
where the time goes:
time: 682 us; the launch traced here: 672 us
  waiting for transfers between devices  292 us (43%)
  local copies, waits for them, and re-layouts  167 us (24%)
  blocking collectives  118 us (17%)
  matrix products  45.5 us (7%)
  other arithmetic  20.5 us (3%)
  between operations  15.7 us (2%)
  starting transfers between devices  13.6 us (2%)
    psum x1, waiting for transfers between devices, shards(): lax.psum((g_query, g_key, g_value, g_out), 'slab')  106 us
    psum x1, waiting for transfers between devices, shards(): g_lift, g_proj, loss = lax.psum((g_lift, g_proj, loss_part), ('slab', 'mp'))  81.8 us
    psum x1, blocking collectives, shards(): g_lift, g_proj, loss = lax.psum((g_lift, g_proj, loss_part), ('slab', 'mp'))  65.5 us
    reshape x2, local copies, waits for them, and re-layouts, cut_patches(): field.reshape(comps, size_z // 8, 8, size_y // 8, 8, size_x // 8, 8)  62.4 us
    transpose x2, local copies, waits for them, and re-layouts, cut_patches(): return blocks.transpose(1, 3, 5, 0, 2, 4, 6).reshape(-1, comps * 512)  45.4 us
    reduce_scatter x1, waiting for transfers between devices, shards(): lax.psum_scatter(jnp.einsum('ta,da->td', rows, weights, preferred_element...  41.8 us
    all_gather x1, waiting for transfers between devices, shards(): lax.all_gather(d_hidden.astype(jnp.bfloat16), 'mp', axis=0, tiled=True)  29.3 us
    all_to_all x1, blocking collectives, shards(): lax.all_to_all(send_old, 'slab', split_axis=0, concat_axis=0, tiled=True)  28.1 us
  transfers between devices with their start and end apart: 11, of which 10 were waited for; matrix products, arithmetic and copies ran while one was open for 17% of the time, Pallas kernels for 0%

commit v1 on v0

--- a/solution.py
+++ b/solution.py
@@ -176,7 +176,7 @@
     g_out = g_out_turned.T
     g_lift = jnp.einsum("tf,td->fd", recv_old, d_lifted, preferred_element_type=jnp.float32)
     g_query, g_key, g_value, g_out = lax.psum((g_query, g_key, g_value, g_out), "slab")
-    g_lift, g_proj, loss = lax.psum((g_lift, g_proj, loss_part), ("slab", "mp"))
+    g_lift, g_proj, loss = lax.psum(lax.psum((g_lift, g_proj, loss_part), "slab"), "mp")
     slab_at = lax.axis_index("slab")
     lift_rows = g_lift.shape[0] // groups
     proj_rows = g_proj.shape[0] // groups

time: 682 us -> 662 us (0.971)
  waiting for transfers between devices: 292 us -> 281 us
    psum x1 -> x2, blocking collectives: 65.5 us -> 63.3 us  [the longest x1 51.7 us: shards(): lax.psum((g_lift, g_proj, loss_part), 'slab')]
  transfers between devices with their start and end apart: 11 -> 11, of which waited for: 10 -> 10; matrix products, arithmetic and copies ran while one was open for 17% -> 16% of each run, Pallas kernels for 0% -> 0%
where the time goes in v1:
time: 662 us; the launch traced here: 651 us
  waiting for transfers between devices  281 us (42%)
  local copies, waits for them, and re-layouts  164 us (25%)
  blocking collectives  115 us (17%)
  matrix products  41.2 us (6%)
  other arithmetic  20.4 us (3%)
  between operations  15.7 us (2%)
  starting transfers between devices  13.3 us (2%)
    psum x1, waiting for transfers between devices, shards(): lax.psum((g_lift, g_proj, loss_part), 'slab')  119 us
    psum x1, waiting for transfers between devices, shards(): lax.psum(lax.psum((g_lift, g_proj, loss_part), 'slab'), 'mp')  64.7 us
    reshape x2, local copies, waits for them, and re-layouts, cut_patches(): field.reshape(comps, size_z // 8, 8, size_y // 8, 8, size_x // 8, 8)  62.5 us
    psum x1, blocking collectives, shards(): lax.psum((g_lift, g_proj, loss_part), 'slab')  51.7 us
    transpose x2, local copies, waits for them, and re-layouts, cut_patches(): return blocks.transpose(1, 3, 5, 0, 2, 4, 6).reshape(-1, comps * 512)  45.4 us
    reduce_scatter x1, waiting for transfers between devices, shards(): lax.psum_scatter(jnp.einsum('ta,da->td', rows, weights, preferred_element...  35.5 us
    all_gather x1, waiting for transfers between devices, shards(): lax.all_gather(d_hidden.astype(jnp.bfloat16), 'mp', axis=0, tiled=True)  29.3 us
    all_to_all x1, blocking collectives, shards(): lax.all_to_all(send_old, 'slab', split_axis=0, concat_axis=0, tiled=True)  28.1 us
  transfers between devices with their start and end apart: 11, of which 10 were waited for; matrix products, arithmetic and copies ran while one was open for 16% of the time, Pallas kernels for 0%

profile of v1, /device:TPU:6, one launch (start us, length us, event | category | flops | bytes accessed | tf_op | source)
XLA Modules:
  0.0 650.5 jit_solution(13516226872149102004)
XLA Ops:
  7.2 2.1 fusion.47
  13.0 3.5 collective-permute-done
  17.3 5.0 fusion.44
  22.3 30.4 %reshape.376 = bf16[3,1,8,16,8,32,8]{6,5,4,3,2,0,1:T(8,128)(2,1)} reshape(bf16[3,8,128,256]{3,2,1,0:T(8,128)(2,1)S(1)} %get-tuple-element.24) | data formatting | bytes 3145728 | tf_op jit(solution)/shard_map/reshape | solution.py:38
  52.8 22.7 %copy.29 = bf16[1,16,32,3,8,8,8]{2,1,6,5,4,3,0:T(8,128)(2,1)} copy(bf16[1,16,32,3,8,8,8]{6,2,5,1,4,3,0:T(8,128)(2,1)} %bitcast.157) | data formatting | bytes 3145728 | tf_op jit(solution)/shard_map/transpose | solution.py:39
  75.5 8.4 %reshape.377 = bf16[512,1536]{0,1:T(8,128)(2,1)S(1)} reshape(bf16[1,16,32,3,8,8,8]{2,1,6,5,4,3,0:T(8,128)(2,1)} %copy.29) | data formatting | bytes 3145728 | tf_op jit(solution)/shard_map/reshape | solution.py:39
  83.8 1.6 copy.30
  85.4 5.3 scatter_custom_fusion
  90.8 28.1 %all_to_all.34 = bf16[32,16,1536]{2,1,0:T(8,128)(2,1)S(1)} all-to-all(bf16[32,16,1536]{2,1,0:T(8,128)(2,1)S(1)} %bitcast.164), channel_id=1, replica_groups=mesh['slab'=32,'mp'=4] {'slab'}, dimensions={0} | all-to-all | bytes 3145728 | tf_op jit(solution)/shard_map/all_to_all | solution.py:97
  120.0 1.8 convolution_convert_fusion.3
  121.8 2.2 scatter_custom_fusion.1
  124.1 11.3 %all_to_all.35 = bf16[32,16,1]{1,2,0:T(2,128)(2,1)S(1)} all-to-all(bf16[32,16,1]{1,2,0:T(2,128)(2,1)S(1)} %all_to_all.30), channel_id=1, replica_groups=mesh['slab'=32,'mp'=4] {'slab'}, dimensions={0} | all-to-all | bytes 2048 | tf_op jit(solution)/shard_map/all_to_all | solution.py:99
  135.5 12.7 %all-gather = bf16[4,1,512]{2,1,0:T(2,128)(2,1)S(1)} all-gather(bf16[1,1,512]{2,1,0:T(2,128)(2,1)S(1)} %reshape.428), channel_id=1, replica_groups=mesh['slab'=32,'mp'=4] {'mp'}, dimensions={0}, use_global_device_ids=true | all-gather | bytes 5120 | tf_op jit(solution)/shard_map/all_gather | solution.py:105
  149.5 4.3 all-gather.4.cloned.1.call-done
  153.7 2.6 convolution_convert_fusion.2
  160.1 1.4 convolution_divide_fusion.1
  162.2 2.7 fusion.49
  165.1 4.1 fusion.45
  173.5 1.4 collective-permute-start.3
  175.3 1.9 collective-permute-done.2
  177.2 2.3 collective-permute-done.3
  179.5 9.0 %fusion.42 = (bf16[3,8,128,256]{3,2,1,0:T(8,128)(2,1)}, f32[3,8,128,256]{3,2,1,0:T(8,128)}) fusion(f32[3,8,128,256]{3,2,1,0:T(8,128)S(1)} %copy-done.1, f32[8,128,256]{2,1,0:T(8,128)S(1)} %get-tuple-element.31, f32[3,1,128,256]{3,2,1,0:T(8,128)S(1)} %collective-permute-done, f32[3,1,128,256]{3,2,1,0:T(8,128)} %copy-done.19, ...), kind=kLoop, calls=%fused_computation.120 | loop fusion | flops 20447232 | bytes 22081536 | tf_op jit(solution)/shard_map/convert_element_type | solution.py:79
  188.5 32.0 %reshape.381 = bf16[3,1,8,16,8,32,8]{6,5,4,3,2,0,1:T(8,128)(2,1)} reshape(bf16[3,8,128,256]{3,2,1,0:T(8,128)(2,1)} %get-tuple-element.20) | data formatting | bytes 3145728 | tf_op jit(solution)/shard_map/reshape | solution.py:38
  220.6 22.7 %copy.33 = bf16[1,16,32,3,8,8,8]{2,1,6,5,4,3,0:T(8,128)(2,1)} copy(bf16[1,16,32,3,8,8,8]{6,2,5,1,4,3,0:T(8,128)(2,1)} %bitcast.158) | data formatting | bytes 3145728 | tf_op jit(solution)/shard_map/transpose | solution.py:39
  243.3 9.3 %reshape.382 = bf16[512,1536]{0,1:T(8,128)(2,1)} reshape(bf16[1,16,32,3,8,8,8]{2,1,6,5,4,3,0:T(8,128)(2,1)} %copy.33) | data formatting | bytes 3145728 | tf_op jit(solution)/shard_map/reshape | solution.py:39
  252.6 2.6 copy.34
  255.2 6.3 scatter_custom_fusion.2
  261.5 10.4 %all-to-all-start.2 = ((bf16[32,16,1536]{2,1,0:T(8,128)(2,1)}), bf16[32,16,1536]{2,1,0:T(8,128)(2,1)}, u32[]{:S(2)}, u32[]{:S(2)}) async-start(bf16[32,16,1536]{2,1,0:T(8,128)(2,1)} %bitcast.163), calls=%async_computation.3 | async-start | bytes 3145728 | tf_op jit(solution)/shard_map/all_to_all | solution.py:98
  272.3 19.5 %all-to-all-done.2 = bf16[32,16,1536]{2,1,0:T(8,128)(2,1)} async-done(((bf16[32,16,1536]{2,1,0:T(8,128)(2,1)}), bf16[32,16,1536]{2,1,0:T(8,128)(2,1)}, u32[]{:S(2)}, u32[]{:S(2)}) %all-to-all-start.2) | async-done | bytes 1572896 | tf_op jit(solution)/shard_map/all_to_all | solution.py:98
  291.8 3.6 multiply_reduce_fusion
  295.4 2.2 fusion.48
  297.7 29.3 %all-gather.6.cloned.1.call-done = bf16[2048,512]{1,0:T(8,128)(2,1)} async-done(((bf16[512,512]{1,0:T(8,128)(2,1)}), bf16[2048,512]{1,0:T(8,128)(2,1)}) %all-gather.6.cloned.1.call-update) | async-done | bytes 2097168 | tf_op jit(solution)/shard_map/all_gather | solution.py:142
  327.0 2.5 fusion.50
  329.6 1.3 convolution_divide_fusion
  335.3 3.3 fusion.3
  339.6 5.1 fusion.19
  344.6 1.2 fusion.54
  345.8 1.4 fusion.51
  347.3 1.4 fusion.53
  348.7 1.4 fusion.52
  350.2 35.5 %reduce-scatter.5.cloned.1.call-done = f32[512,512]{1,0:T(8,128)} async-done(((f32[2048,512]{1,0:T(8,128)}), f32[512,512]{1,0:T(8,128)}) %reduce-scatter.5.cloned.1.call-update) | async-done | bytes 1048592 | tf_op jit(solution)/shard_map/reduce_scatter | solution.py:169
  385.6 4.3 fusion.21
  390.0 118.8 %all-reduce.5.cloned.1.call-done = (f32[1536,512]{1,0:T(8,128)}, f32[512,128]{1,0:T(8,128)}, f32[512,128]{1,0:T(8,128)}, f32[512,128]{1,0:T(8,128)}, f32[128,512]{1,0:T(8,128)}, /*index=5*/f32[512,1536]{1,0:T(8,128)}) async-done(((f32[1536,512]{1,0:T(8,128)}, f32[512,128]{1,0:T(8,128)}, f32[512,128]{1,0:T(8,128)}, f32[512,128]{1,0:T(8,128)}, f32[128,512]{1,0:T(8,128)}, /*index=5*/f32[512,1536]{1,0:T(8,128)}), ...) | async-done | bytes 7340048 | tf_op jit(solution)/shard_map/psum | solution.py:179
  509.6 51.7 %psum.70 = f32[]{:T(128)} all-reduce(f32[]{:T(128)S(6)} %div.119), channel_id=1, replica_groups=mesh['slab'=32,'mp'=4] {'slab'}, use_global_device_ids=true, to_apply=%region_13.14 | all-reduce | flops 1 | bytes 8 | tf_op jit(solution)/shard_map/psum | solution.py:179
  561.3 11.6 %psum.71 = f32[]{:T(128)} all-reduce(f32[]{:T(128)} %psum.70), channel_id=1, replica_groups=mesh['slab'=32,'mp'=4] {'mp'}, use_global_device_ids=true, to_apply=%region_14.15 | all-reduce | flops 1 | bytes 8 | tf_op jit(solution)/shard_map/psum | solution.py:179
  572.9 64.7 %all-reduce.7.cloned.1.call-done = (f32[1536,512]{1,0:T(8,128)}, f32[512,1536]{1,0:T(8,128)}) async-done(((f32[1536,512]{1,0:T(8,128)}, f32[512,1536]{1,0:T(8,128)}), (f32[1536,512]{1,0:T(8,128)}, f32[512,1536]{1,0:T(8,128)})) %all-reduce.7.cloned.1.call-update) | async-done | bytes 6291472 | tf_op jit(solution)/shard_map/psum | solution.py:179
  637.6 1.5 constant_dynamic-slice_fusion.1
  639.1 1.5 constant_dynamic-slice_fusion
  (164 shorter events, 25.0 us)
Async XLA Ops:
  7.2 284.6 %copy-start = (bf16[512,1536]{1,0:T(8,128)(2,1)S(1)}, bf16[512,1536]{1,0:T(8,128)(2,1)}, u32[]{:S(2)}) copy-start(bf16[512,1536]{1,0:T(8,128)(2,1)} %param.17) | copy-start | bytes 4718596
  7.2 146.6 %all-gather.4.cloned.1.call-start = ((), (), s32[]{:S(2)}) async-start(), calls=%async_computation.5 | async-start | bytes 2621440 | tf_op jit(solution)/shard_map/all_gather | solution.py:104
  9.3 7.2 %collective-permute-start = (f32[3,1,128,256]{3,2,1,0:T(8,128)S(1)}, f32[3,1,128,256]{3,2,1,0:T(8,128)S(1)}, u32[]{:S(2)}, u32[]{:S(2)}) collective-permute-start(f32[3,1,128,256]{3,2,1,0:T(8,128)S(1)} %get-tuple-element.34), channel_id=1, source_target_pairs={{0,4},{4,8},{8,12},{12,16},{16,20},{20,24},{24,28},{28,32},{32,36}... | collective-permute-start | bytes 1179656 | tf_op jit(solution)/shard_map/ppermute | solution.py:20
  10.0 75.4 %copy-start.48 = (s32[1024]{0:T(1024)}, s32[1024]{0:T(1024)S(1)}, u32[]{:S(2)}) copy-start(s32[1024]{0:T(1024)S(1)} %pad_clamp_fusion) | copy-start | bytes 12292
  13.0 108.8 %copy-start.49 = (s32[256,1]{0,1:T(1,128)}, s32[256,1]{0,1:T(1,128)S(1)}, u32[]{:S(2)}) copy-start(s32[256,1]{0,1:T(1,128)S(1)} %compare_select_fusion.1) | copy-start | bytes 3076
  90.8 29.2 %copy-start.50 = (bf16[1536,512]{1,0:T(8,128)(2,1)S(1)}, bf16[1536,512]{1,0:T(8,128)(2,1)}, u32[]{:S(2)}) copy-start(bf16[1536,512]{1,0:T(8,128)(2,1)} %param.12) | copy-start | bytes 4718596
  118.8 34.9 %copy-start.44 = (bf16[512,128]{1,0:T(8,128)(2,1)S(1)}, bf16[512,128]{1,0:T(8,128)(2,1)}, u32[]{:S(2)}) copy-start(bf16[512,128]{1,0:T(8,128)(2,1)} %param.13) | copy-start | bytes 393220
  120.0 36.4 %copy-start.42 = (bf16[512,128]{1,0:T(8,128)(2,1)S(1)}, bf16[512,128]{1,0:T(8,128)(2,1)}, u32[]{:S(2)}) copy-start(bf16[512,128]{1,0:T(8,128)(2,1)} %param.14) | copy-start | bytes 393220
  121.8 170.0 %reduce-scatter.3.cloned.1.call-start = ((), (), s32[]{:S(2)}) async-start(), calls=%async_computation.6 | async-start | bytes 5242880 | tf_op jit(solution)/shard_map/reduce_scatter | solution.py:129
  135.3 21.0 %copy-start.38 = (bf16[32,16,1]{1,2,0:T(2,128)(2,1)}, bf16[32,16,1]{1,2,0:T(2,128)(2,1)S(1)}, u32[]{:S(2)}) copy-start(bf16[32,16,1]{1,2,0:T(2,128)(2,1)S(1)} %all_to_all.35) | copy-start | bytes 3076
  153.7 2.6 copy-start.2
  156.3 5.2 copy-start.10
  159.0 3.2 copy-start.24
  159.1 3.1 copy-start.26
  160.0 2.2 copy-start.36
  160.1 2.1 copy-start.22
  164.9 4.3 copy-start.1
  164.9 5.8 collective-permute-start.1
  170.7 2.8 copy-start.19
  172.7 4.5 collective-permute-start.2
  173.5 6.0 collective-permute-start.3
  255.2 16.9 %copy-start.39 = (bf16[32,16,1]{1,2,0:T(2,128)(2,1)S(1)}, bf16[32,16,1]{1,2,0:T(2,128)(2,1)}, u32[]{:S(2)}) copy-start(bf16[32,16,1]{1,2,0:T(2,128)(2,1)} %copy-done.38) | copy-start | bytes 3076
  261.5 30.3 %all-to-all-start.2 = ((bf16[32,16,1536]{2,1,0:T(8,128)(2,1)}), bf16[32,16,1536]{2,1,0:T(8,128)(2,1)}, u32[]{:S(2)}, u32[]{:S(2)}) async-start(bf16[32,16,1536]{2,1,0:T(8,128)(2,1)} %bitcast.163), calls=%async_computation.3 | async-start | bytes 3145728 | tf_op jit(solution)/shard_map/all_to_all | solution.py:98
  271.8 55.2 %all-gather.6.cloned.1.call-start = ((), (), s32[]{:S(2)}) async-start(), calls=%async_computation.7 | async-start | bytes 2621440 | tf_op jit(solution)/shard_map/all_gather | solution.py:142
  295.4 2.2 copy-start.4
  295.4 31.6 %copy-start.25 = (bf16[128,512]{1,0:T(8,128)(2,1)S(1)}, bf16[128,512]{1,0:T(8,128)(2,1)}, u32[]{:S(2)}) copy-start(bf16[128,512]{1,0:T(8,128)(2,1)} %param.16) | copy-start | bytes 393220
  297.6 33.3 %copy-start.29 = (f32[2,64,64]{2,1,0:T(8,128)S(1)}, f32[2,64,64]{2,1,0:T(8,128)}, u32[]{:S(2)}) copy-start(f32[2,64,64]{2,1,0:T(8,128)} %copy-done.28) | copy-start | bytes 98308
  297.7 34.3 %copy-start.27 = (f32[2048,2]{0,1:T(2,128)S(1)}, f32[2048,2]{0,1:T(2,128)}, u32[]{:S(2)}) copy-start(f32[2048,2]{0,1:T(2,128)} %copy-done.26) | copy-start | bytes 49156
  297.7 34.3 %copy-start.37 = (f32[2048,2]{0,1:T(2,128)S(1)}, f32[2048,2]{0,1:T(2,128)}, u32[]{:S(2)}) copy-start(f32[2048,2]{0,1:T(2,128)} %copy-done.36) | copy-start | bytes 49156
  297.7 34.3 %copy-start.47 = (f32[4,1,512]{2,1,0:T(1,128)S(1)}, f32[4,1,512]{2,1,0:T(1,128)}, u32[]{:S(2)}) copy-start(f32[4,1,512]{2,1,0:T(1,128)} %compare_convert_fusion.1) | copy-start | bytes 24580
  297.7 87.9 %reduce-scatter.5.cloned.1.call-start = ((), (), s32[]{:S(2)}) async-start(), calls=%async_computation.8 | async-start | bytes 5242880 | tf_op jit(solution)/shard_map/reduce_scatter | solution.py:169
  327.0 2.6 copy-start.11
  327.0 5.0 copy-start.6
  327.0 5.0 copy-start.21
  330.9 2.0 copy-start.23
  332.0 2.4 copy-start.13
  338.5 7.3 %copy-start.14 = (bf16[2,64,2048]{2,1,0:T(8,128)(2,1)S(1)}, bf16[2,64,2048]{2,1,0:T(8,128)(2,1)}, u32[]{:S(2)}) copy-start(bf16[2,64,2048]{2,1,0:T(8,128)(2,1)} %copy-done.13) | copy-start | bytes 1572868
  338.6 170.3 %all-reduce.5.cloned.1.call-start = ((), (), s32[]{:S(2)}) async-start(), calls=%async_computation.9 | async-start | bytes 14680064 | tf_op jit(solution)/shard_map/psum | solution.py:179
  339.6 5.1 copy-start.9
  339.6 6.3 copy-start.3
  344.6 2.6 copy-start.16
  345.8 2.9 copy-start.18
  347.3 38.4 %copy-start.8 = (bf16[32,16,1536]{2,1,0:T(8,128)(2,1)S(1)}, bf16[32,16,1536]{2,1,0:T(8,128)(2,1)}, u32[]{:S(2)}) copy-start(bf16[32,16,1536]{2,1,0:T(8,128)(2,1)} %copy-done.7) | copy-start | bytes 4718596
  390.0 247.6 %all-reduce.7.cloned.1.call-start = ((), (), s32[]{:S(2)}) async-start(), calls=%async_computation.10 | async-start | bytes 12582912 | tf_op jit(solution)/shard_map/psum | solution.py:179
  508.8 131.8 %copy-start.33 = (f32[512,128]{1,0:T(8,128)S(1)}, f32[512,128]{1,0:T(8,128)}, u32[]{:S(2)}) copy-start(f32[512,128]{1,0:T(8,128)} %get-tuple-element.52) | copy-start | bytes 786436
  508.8 132.5 %copy-start.32 = (f32[512,128]{1,0:T(8,128)S(1)}, f32[512,128]{1,0:T(8,128)}, u32[]{:S(2)}) copy-start(f32[512,128]{1,0:T(8,128)} %get-tuple-element.53) | copy-start | bytes 786436
  508.8 133.2 %copy-start.31 = (f32[512,128]{1,0:T(8,128)S(1)}, f32[512,128]{1,0:T(8,128)}, u32[]{:S(2)}) copy-start(f32[512,128]{1,0:T(8,128)} %get-tuple-element.54) | copy-start | bytes 786436
  508.8 133.9 %copy-start.30 = (f32[128,512]{1,0:T(8,128)S(1)}, f32[128,512]{1,0:T(8,128)}, u32[]{:S(2)}) copy-start(f32[128,512]{1,0:T(8,128)} %get-tuple-element.55) | copy-start | bytes 786436
  (14 other events, 18.3 us)
Sparse Core Ops, SparseCore 0:
  121.9 31.8 all-gather.3
  165.0 47.4 reduce-scatter.2
  297.8 29.2 all-gather.5
  338.7 46.9 reduce-scatter.4
  390.1 118.6 all-reduce.4
  511.1 126.4 all-reduce.6
